TPU v7x, 32 devices: a whole 2x2x4 slice. The times are simulated.
32 devices in a mesh: dp: 8 (over z, x), seq: 4 (over y, core).
Axes of the slice: x: 2, y: 2, z: 4, core: 2. Of those that a mesh axis runs over, the one named last changes fastest.
Arguments:
- queries: bfloat16 [8, 512, 32, 128], P('dp', 'seq'), may hold values from -13 to 13
- keys: bfloat16 [8, 512, 4, 128], P('dp', 'seq'), may hold values from -13 to 13
- values: bfloat16 [8, 512, 4, 128], P('dp', 'seq'), may hold values from -6 to 6
- d_out: bfloat16 [8, 512, 32, 128], P('dp', 'seq'), may hold values from -6 to 6
- doc_ids: int32 [8, 512], P('dp', 'seq'), may hold values from 0 to 3, never falling along the last dimension, each value on 1 to 256 neighbouring positions
Outputs:
- query_grad: bfloat16 [8, 512, 32, 128], P('dp', 'seq')
- key_grad: bfloat16 [8, 512, 4, 128], P('dp', 'seq')
- value_grad: bfloat16 [8, 512, 4, 128], P('dp', 'seq')
- value_bias_grad: float32 [512], P('dp')
Inputs may be any that keep to these rules, and one draw needn't show every extreme that they name: `doc_ids`: in each row the ids never fall along the tokens; each of the 4 ids marks one document of 1 to 256 tokens, and one document has exactly 256.
All inputs are finite; a program needn't handle non-finite values.
Results may differ from a plain program's by a relative error of at most 0.0073.
Values may be sent and summed in bfloat16 or wider, within the bound.
No kernel may reach another device: no remote copies, remote signals or barrier semaphores. Data moves between devices by JAX's collectives and lax.ppermute only.
A program may use at most 64 MiB of HBM per device.

v0:
```python
import math
import jax
import jax.numpy as jnp
from jax import lax
from jax.sharding import PartitionSpec as P

masked_score = -1e30


def tile_terms(
    query_block,
    grad_block,
    block_of_keys,
    block_of_values,
    query_docs,
    key_docs,
    query_first,
    key_first,
    score_scale,
):
    scores = (
        jnp.einsum("qhd,kd->hqk", query_block, block_of_keys, preferred_element_type=jnp.float32)
        * score_scale
    )
    dweights = jnp.einsum(
        "qhd,kd->hqk", grad_block, block_of_values, preferred_element_type=jnp.float32
    )
    rows_per_block = query_block.shape[0]
    query_place = query_first + jnp.arange(rows_per_block)
    key_place = key_first + jnp.arange(rows_per_block)
    allowed = (key_place[None, :] <= query_place[:, None]) & (
        key_docs[None, :] == query_docs[:, None]
    )
    masked = jnp.where(allowed[None], scores, masked_score)
    return (masked, dweights, allowed)


def shards(queries, keys, values, d_out, doc_ids):
    seq_size = lax.axis_size("seq")
    query_local = queries[0]
    grad_local = d_out[0]
    key_local = keys[0]
    value_local = values[0]
    kv_heads = key_local.shape[1]
    head_dim = key_local.shape[2]
    local_tokens = query_local.shape[0]
    head_copies = seq_size // kv_heads
    documents_per_row = lax.all_gather(doc_ids[0], "seq", axis=0, tiled=True)
    query_row, grad_row = (
        lax.all_to_all(query_local, "seq", split_axis=1, concat_axis=0, tiled=True),
        lax.all_to_all(grad_local, "seq", split_axis=1, concat_axis=0, tiled=True),
    )
    key_copies, value_copies = (
        lax.all_to_all(
            jnp.repeat(key_local, head_copies, axis=1),
            "seq",
            split_axis=1,
            concat_axis=0,
            tiled=True,
        ),
        lax.all_to_all(
            jnp.repeat(value_local, head_copies, axis=1),
            "seq",
            split_axis=1,
            concat_axis=0,
            tiled=True,
        ),
    )
    row_of_keys = key_copies[:, 0]
    row_of_values = value_copies[:, 0]
    row_length = query_row.shape[0]
    local_heads = query_row.shape[1]
    rows_per_block = min(512, row_length)
    block_count = row_length // rows_per_block
    score_scale = 1.0 / math.sqrt(head_dim)
    doc_blocks = documents_per_row.reshape(block_count, rows_per_block)
    lowest = jnp.sum((doc_blocks[None, :, -1] < doc_blocks[:, None, 0]).astype(jnp.int32), axis=1)

    def select_block(array, index):
        return lax.dynamic_slice_in_dim(array, index * rows_per_block, rows_per_block, 0)

    def row_stats(qindex):
        query_block = select_block(query_row, qindex)
        grad_block = select_block(grad_row, qindex)
        query_docs = select_block(documents_per_row, qindex)

        def row_tile_step(key_index, running_total):
            row_top, exp_total, weighted = running_total
            masked, dweights, allowed = tile_terms(
                query_block,
                grad_block,
                select_block(row_of_keys, key_index),
                select_block(row_of_values, key_index),
                query_docs,
                select_block(documents_per_row, key_index),
                qindex * rows_per_block,
                key_index * rows_per_block,
                score_scale,
            )
            new_top = jnp.maximum(row_top, jnp.max(masked, axis=2))
            factor = jnp.exp(row_top - new_top)
            exponent = jnp.where(allowed[None], jnp.exp(masked - new_top[:, :, None]), 0.0)
            return (
                new_top,
                exp_total * factor + jnp.sum(exponent, axis=2),
                weighted * factor + jnp.sum(exponent * dweights, axis=2),
            )

        zeros = jnp.zeros((local_heads, rows_per_block), jnp.float32)
        first_state = (
            jnp.full((local_heads, rows_per_block), masked_score, jnp.float32),
            zeros,
            zeros,
        )
        row_top, exp_total, weighted = lax.fori_loop(
            lowest[qindex], qindex + 1, row_tile_step, first_state
        )
        return (row_top, exp_total, weighted / exp_total)

    row_tops, row_totals, row_deltas = lax.map(row_stats, jnp.arange(block_count))

    def backward(qindex, running_total):
        query_all, key_acc, value_acc = running_total
        query_block = select_block(query_row, qindex)
        grad_block = select_block(grad_row, qindex)
        query_docs = select_block(documents_per_row, qindex)
        row_top = row_tops[qindex]
        exp_total = row_totals[qindex]
        row_delta = row_deltas[qindex]

        def backward_tile_step(key_index, inner_product):
            query_acc, key_inner_product, value_inner_product = inner_product
            block_of_keys = select_block(row_of_keys, key_index)
            block_of_values = select_block(row_of_values, key_index)
            masked, dweights, allowed = tile_terms(
                query_block,
                grad_block,
                block_of_keys,
                block_of_values,
                query_docs,
                select_block(documents_per_row, key_index),
                qindex * rows_per_block,
                key_index * rows_per_block,
                score_scale,
            )
            weights = jnp.where(
                allowed[None], jnp.exp(masked - row_top[:, :, None]) / exp_total[:, :, None], 0.0
            )
            dscores = weights * (dweights - row_delta[:, :, None])
            weights_half = weights.astype(jnp.bfloat16)
            dscores_half = dscores.astype(jnp.bfloat16)
            query_acc = query_acc + jnp.einsum(
                "hqk,kd->qhd", dscores_half, block_of_keys, preferred_element_type=jnp.float32
            )
            key_piece = jnp.einsum(
                "hqk,qhd->kd", dscores_half, query_block, preferred_element_type=jnp.float32
            )
            value_piece = jnp.einsum(
                "hqk,qhd->kd", weights_half, grad_block, preferred_element_type=jnp.float32
            )
            key_inner_product = lax.dynamic_update_slice_in_dim(
                key_inner_product,
                select_block(key_inner_product, key_index) + key_piece,
                key_index * rows_per_block,
                0,
            )
            value_inner_product = lax.dynamic_update_slice_in_dim(
                value_inner_product,
                select_block(value_inner_product, key_index) + value_piece,
                key_index * rows_per_block,
                0,
            )
            return (query_acc, key_inner_product, value_inner_product)

        query_start = jnp.zeros((rows_per_block, local_heads, head_dim), jnp.float32)
        query_acc, key_acc, value_acc = lax.fori_loop(
            lowest[qindex], qindex + 1, backward_tile_step, (query_start, key_acc, value_acc)
        )
        query_all = lax.dynamic_update_slice_in_dim(
            query_all, query_acc, qindex * rows_per_block, 0
        )
        return (query_all, key_acc, value_acc)

    start_state = (
        jnp.zeros((row_length, local_heads, head_dim), jnp.float32),
        jnp.zeros((row_length, head_dim), jnp.float32),
        jnp.zeros((row_length, head_dim), jnp.float32),
    )
    query_all, key_acc, value_acc = lax.fori_loop(0, block_count, backward, start_state)
    query_half = (query_all * score_scale).astype(jnp.bfloat16)
    key_half = (key_acc * score_scale).astype(jnp.bfloat16)[:, None]
    value_half = value_acc.astype(jnp.bfloat16)[:, None]
    query_grad, key_back, value_back = (
        lax.all_to_all(query_half, "seq", split_axis=0, concat_axis=1, tiled=True),
        lax.all_to_all(key_half, "seq", split_axis=0, concat_axis=1, tiled=True),
        lax.all_to_all(value_half, "seq", split_axis=0, concat_axis=1, tiled=True),
    )
    summed_key = jnp.sum(
        key_back.reshape(local_tokens, kv_heads, head_copies, head_dim), axis=2, dtype=jnp.float32
    )
    summed_value = jnp.sum(
        value_back.reshape(local_tokens, kv_heads, head_copies, head_dim), axis=2, dtype=jnp.float32
    )
    partial_value = jnp.sum(summed_value, axis=0).reshape(-1)
    row_bias = lax.psum_scatter(partial_value, "dp", scatter_dimension=0, tiled=True)
    total_bias = lax.psum(row_bias, "seq")
    total_tokens = local_tokens * seq_size * lax.axis_size("dp")
    return (
        query_grad[None],
        summed_key.astype(jnp.bfloat16)[None],
        summed_value.astype(jnp.bfloat16)[None],
        total_bias / math.sqrt(total_tokens),
    )


def solution(mesh):
    placed = (
        P("dp", "seq", None, None),
        P("dp", "seq", None, None),
        P("dp", "seq", None, None),
        P("dp", "seq", None, None),
        P("dp", "seq"),
    )
    return jax.shard_map(
        shards,
        mesh=mesh,
        in_specs=placed,
        out_specs=(
            P("dp", "seq", None, None),
            P("dp", "seq", None, None),
            P("dp", "seq", None, None),
            P("dp"),
        ),
        check_vma=False,
    )
```

profile of v0, /device:TPU:0, one launch (start us, length us, event | category | flops | bytes accessed | tf_op | source)
XLA Modules:
  0.0 128.4 jit_solution(110084953796103875)
XLA Ops:
  0.7 1.6 %copy.62 = bf16[1,128,4,128]{3,1,2,0:T(8,128)(2,1)} copy(bf16[1,128,4,128]{3,2,1,0:T(4,128)(2,1)} %param.10) | data formatting | bytes 262144 | tf_op args[1]
  2.3 4.3 %all-to-all-start = ((bf16[128,4,128]{2,0,1:T(8,128)(2,1)}), bf16[128,4,128]{2,0,1:T(8,128)(2,1)S(1)}, u32[]{:S(2)}, u32[]{:S(2)}) async-start(bf16[128,4,128]{2,0,1:T(8,128)(2,1)} %bitcast.125), calls=%async_computation | async-start | bytes 262144 | tf_op jit(solution)/shard_map/all_to_all | solution.py:54
  6.5 2.6 %copy.60 = bf16[1,128,32,128]{3,1,2,0:T(8,128)(2,1)} copy(bf16[1,128,32,128]{3,2,1,0:T(8,128)(2,1)} %param.9) | data formatting | bytes 2097152 | tf_op args[0]
  9.1 2.0 %all-to-all-done = bf16[128,4,128]{2,0,1:T(8,128)(2,1)S(1)} async-done(((bf16[128,4,128]{2,0,1:T(8,128)(2,1)}), bf16[128,4,128]{2,0,1:T(8,128)(2,1)S(1)}, u32[]{:S(2)}, u32[]{:S(2)}) %all-to-all-start) | async-done | bytes 131104 | tf_op jit(solution)/shard_map/all_to_all | solution.py:54
  11.1 3.5 %all-to-all-start.1 = ((bf16[128,32,128]{2,0,1:T(8,128)(2,1)}), bf16[128,32,128]{2,0,1:T(8,128)(2,1)S(1)}, u32[]{:S(2)}, u32[]{:S(2)}) async-start(bf16[128,32,128]{2,0,1:T(8,128)(2,1)} %bitcast.123), calls=%async_computation.1 | async-start | bytes 2097152 | tf_op jit(solution)/shard_map/all_to_all | solution.py:50
  14.7 2.6 %copy.59 = bf16[1,128,32,128]{3,1,2,0:T(8,128)(2,1)} copy(bf16[1,128,32,128]{3,2,1,0:T(8,128)(2,1)} %param.12) | data formatting | bytes 2097152 | tf_op args[3]
  17.3 11.8 %all-to-all-done.1 = bf16[128,32,128]{2,0,1:T(8,128)(2,1)S(1)} async-done(((bf16[128,32,128]{2,0,1:T(8,128)(2,1)}), bf16[128,32,128]{2,0,1:T(8,128)(2,1)S(1)}, u32[]{:S(2)}, u32[]{:S(2)}) %all-to-all-start.1) | async-done | bytes 1048608 | tf_op jit(solution)/shard_map/all_to_all | solution.py:50
  29.1 3.5 %all-to-all-start.3 = ((bf16[128,32,128]{2,0,1:T(8,128)(2,1)}), bf16[128,32,128]{2,0,1:T(8,128)(2,1)S(1)}, u32[]{:S(2)}, u32[]{:S(2)}) async-start(bf16[128,32,128]{2,0,1:T(8,128)(2,1)} %bitcast.122), calls=%async_computation.3 | async-start | bytes 2097152 | tf_op jit(solution)/shard_map/all_to_all | solution.py:51
  33.3 14.6 %all-gather = s32[1,512]{1,0:T(1,128)S(1)} all-gather(s32[1,128]{1,0:T(1,128)S(1)} %copy-done.3), channel_id=2, replica_groups=mesh['dp'=8,'seq'=4] {'seq'}, dimensions={1}, use_global_device_ids=true | all-gather | bytes 2560 | tf_op jit(solution)/shard_map/all_gather | solution.py:48
  47.9 3.3 %all-to-all-start.2 = ((bf16[128,4,128]{2,0,1:T(8,128)(2,1)}), bf16[128,4,128]{2,0,1:T(8,128)(2,1)S(1)}, u32[]{:S(2)}, u32[]{:S(2)}) async-start(bf16[128,4,128]{2,0,1:T(8,128)(2,1)} %bitcast.124), calls=%async_computation.2 | async-start | bytes 262144 | tf_op jit(solution)/shard_map/all_to_all | solution.py:61
  53.3 2.5 %all-to-all-done.2 = bf16[128,4,128]{2,0,1:T(8,128)(2,1)S(1)} async-done(((bf16[128,4,128]{2,0,1:T(8,128)(2,1)}), bf16[128,4,128]{2,0,1:T(8,128)(2,1)S(1)}, u32[]{:S(2)}, u32[]{:S(2)}) %all-to-all-start.2) | async-done | bytes 131104 | tf_op jit(solution)/shard_map/all_to_all | solution.py:61
  55.8 6.9 %while.59 = (s32[]{:T(128)}, f32[8,512]{1,0:T(8,128)S(1)}, f32[8,512]{1,0:T(8,128)S(1)}, f32[8,512]{1,0:T(8,128)S(1)}, s32[512]{0:T(512)S(1)}, /*index=5*/bf16[5...) while((s32[]{:T(128)}, f32[8,512]{1,0:T(8,128)S(1)}, ...), condition=%wide.region_4.0_spmd, body=%wide.region_0.4_spmd.sunk | while | flops 1103901184 | bytes 28874876 | solution.py:115
  56.1 1.5 %fusion.63 = (f32[8,512]{1,0:T(8,128)S(1)}, f32[512,512,8]{1,0,2:T(8,128)S(1)}) fusion(pred[512,512]{0,1:T(8,128)(4,1)S(1)} %fusion.62, bf16[512,8,128]{2,0,1:T(8,128)(2,1)S(1)} %get-tuple-element.748, bf16[512,128]{1,0:T(8,128)(2,1)S(1)} %get-tuple-element.747), kind=kOutput, calls=%fused_computation.4.clone.1 | convolution fusion | flops 543158272 | bytes 9846784 | tf_op jit(solution)/shard_map/while/body/eval_jaxpr/while/body/qhd,kd->hqk/dot_general | solution.py:22
  57.7 2.0 %fusion.65 = f32[8,512]{1,0:T(8,128)S(1)} fusion(f32[512,512,8]{1,0,2:T(8,128)S(1)} %get-tuple-element.705, f32[8,512]{1,0:T(8,128)S(1)} %max.9, pred[512,512]{0,1:T(8,128)(4,1)S(1)} %fusion.62), kind=kLoop, calls=%fused_computation.5.clone.1 | loop fusion | flops 10481664 | bytes 8683520 | tf_op jit(solution)/shard_map/while/body/eval_jaxpr/while/body/reduce_sum | solution.py:105
  59.7 3.0 %fusion.64 = f32[8,512]{1,0:T(8,128)S(1)} fusion(f32[512,512,8]{1,0,2:T(8,128)S(1)} %get-tuple-element.705, f32[8,512]{1,0:T(8,128)S(1)} %max.9, pred[512,512]{0,1:T(8,128)(4,1)S(1)} %fusion.62, bf16[512,8,128]{2,0,1:T(8,128)(2,1)S(1)} %get-tuple-element.750, bf16[512,128]{1,0:T(8,128)(2,1)S(1)} %get-tuple-element.749), kind=kOutput, calls=%fused_computation.1.clone.1 | convolution fusion | flops 549449728 | bytes 9863168 | tf_op jit(solution)/shard_map/while/body/eval_jaxpr/while/body/qhd,kd->hqk/dot_general | solution.py:25
  62.8 1.5 %broadcast.192 = f32[512,8,128]{2,0,1:T(8,128)} broadcast(f32[]{:T(128)} %constant.131.clone.1), dimensions={} | broadcast | bytes 2097156 | tf_op jit(solution)/shard_map/broadcast.14
  64.3 10.2 %while.60 = (s32[]{:T(128)}, f32[512,8,128]{2,0,1:T(8,128)}, f32[512,128]{1,0:T(8,128)S(1)}, f32[512,128]{1,0:T(8,128)S(1)}, s32[512]{0:T(512)S(1)}, /*index=5*/...) while((s32[]{:T(128)}, f32[512,8,128]{2,0,1:T(8,128)}, ...), condition=%wide.region_6.7_spmd, body=%wide.region_5.0_spmd.sunk | while | flops 2704671232 | bytes 64936140 | solution.py:176
  64.6 2.9 %fusion.77 = f32[8,512,512]{1,2,0:T(8,128)S(1)} fusion(f32[8,512]{1,0:T(8,128)S(1)} %bitcast.190, f32[8,512]{1,0:T(8,128)S(1)} %bitcast.184, pred[512,512]{0,1:T(8,128)(4,1)S(1)} %fusion.76, bf16[512,8,128]{2,0,1:T(8,128)(2,1)S(1)} %get-tuple-element.787, bf16[512,128]{1,0:T(8,128)(2,1)S(1)} %get-tuple-element.786), kind=kOutput, calls=%fused_computation.22.clone.1 | convolution fusion | flops 547356672 | bytes 9863168 | tf_op jit(solution)/shard_map/while/body/eval_jaxpr/while/body/qhd,kd->hqk/dot_general | solution.py:22
  67.5 1.3 %fusion.80 = f32[512,128]{1,0:T(8,128)S(1)} fusion(f32[512,128]{1,0:T(8,128)S(1)} %get-tuple-element.770, bf16[512,8,128]{2,0,1:T(8,128)(2,1)S(1)} %get-tuple-element.791, f32[8,512,512]{1,2,0:T(8,128)S(1)} %fusion.77), kind=kOutput, calls=%fused_computation.28.clone.1 | convolution fusion | flops 539033600 | bytes 9961472 | tf_op jit(solution)/shard_map/while/body/eval_jaxpr/while/body/hqk,qhd->kd/dot_general | solution.py:158
  68.9 1.3 %fusion.78 = bf16[8,512,512]{1,2,0:T(8,128)(2,1)S(1)} fusion(f32[8,512,512]{1,2,0:T(8,128)S(1)} %fusion.77, f32[8,512]{1,0:T(8,128)S(1)} %bitcast.191, bf16[512,8,128]{2,0,1:T(8,128)(2,1)S(1)} %get-tuple-element.791, bf16[512,128]{1,0:T(8,128)(2,1)S(1)} %get-tuple-element.790), kind=kOutput, calls=%fused_computation.17.clone.1 | convolution fusion | flops 543162368 | bytes 13778944 | tf_op jit(solution)/shard_map/while/body/eval_jaxpr/while/body/qhd,kd->hqk/dot_general | solution.py:25
  70.2 1.3 fusion.79
  71.5 1.7 %bitcast_add_fusion.2 = f32[512,8,128]{2,0,1:T(8,128)S(1)} fusion(f32[512,8,128]{2,0,1:T(8,128)S(1)} %copy-done, bf16[8,512,512]{1,2,0:T(8,128)(2,1)S(1)} %fusion.78, bf16[512,128]{1,0:T(8,128)(2,1)S(1)} %get-tuple-element.786), kind=kOutput, calls=%fused_computation.25.clone.1 | convolution fusion | flops 537395200 | bytes 8519680 | tf_op jit(solution)/shard_map/while/body/eval_jaxpr/while/body/hqk,kd->qhd/dot_general | solution.py:152
  73.2 1.3 %copy-done.1 = f32[512,8,128]{2,0,1:T(8,128)} copy-done((f32[512,8,128]{2,0,1:T(8,128)}, f32[512,8,128]{2,0,1:T(8,128)S(1)}, u32[]{:S(2)}) %copy-start.1) | copy-done | bytes 2097176 | tf_op jit(solution)/shard_map/while/body/eval_jaxpr/while
  76.4 3.3 %all-to-all-start.5 = ((bf16[4,2,8192]{2,1,0:T(2,128)(2,1)}), bf16[4,2,8192]{2,1,0:T(2,128)(2,1)S(1)}, u32[]{:S(2)}, u32[]{:S(2)}) async-start(bf16[4,2,8192]{2,1,0:T(2,128)(2,1)} %reshape.211), calls=%async_computation.5 | async-start | bytes 262144 | tf_op jit(solution)/shard_map/all_to_all | solution.py:195
  81.1 3.2 %all-to-all-done.5 = bf16[4,2,8192]{2,1,0:T(2,128)(2,1)S(1)} async-done(((bf16[4,2,8192]{2,1,0:T(2,128)(2,1)}), bf16[4,2,8192]{2,1,0:T(2,128)(2,1)S(1)}, u32[]{:S(2)}, u32[]{:S(2)}) %all-to-all-start.5) | async-done | bytes 131104 | tf_op jit(solution)/shard_map/all_to_all | solution.py:195
  84.3 3.3 %all-to-all-start.6 = ((bf16[4,2,8192]{2,1,0:T(2,128)(2,1)}), bf16[4,2,8192]{2,1,0:T(2,128)(2,1)S(1)}, u32[]{:S(2)}, u32[]{:S(2)}) async-start(bf16[4,2,8192]{2,1,0:T(2,128)(2,1)} %reshape.213), calls=%async_computation.6 | async-start | bytes 262144 | tf_op jit(solution)/shard_map/all_to_all | solution.py:196
  87.7 3.9 %fusion.26 = bf16[512,8,128]{2,1,0:T(8,128)(2,1)} fusion(f32[512,8,128]{2,0,1:T(8,128)} %get-tuple-element.519), kind=kLoop, calls=%fused_computation.37 | loop fusion | flops 1048576 | bytes 3145728 | tf_op jit(solution)/shard_map/convert_element_type | solution.py:190
  92.2 3.5 %all-to-all-start.4 = ((bf16[512,8,128]{2,1,0:T(8,128)(2,1)}), bf16[512,8,128]{2,1,0:T(8,128)(2,1)S(1)}, u32[]{:S(2)}, u32[]{:S(2)}) async-start(bf16[512,8,128]{2,1,0:T(8,128)(2,1)} %fusion.26), calls=%async_computation.4 | async-start | bytes 2097152 | tf_op jit(solution)/shard_map/all_to_all | solution.py:194
  97.2 0.8 copy.46
  98.9 22.1 %all-reduce = f32[512]{0:T(512)S(1)} all-reduce(f32[512]{0:T(512)S(1)} %bitcast.193), channel_id=3, replica_groups=mesh['dp'=8,'seq'=4] {'dp'}, use_global_device_ids=true, to_apply=%region_8.9.clone | all-reduce | flops 512 | bytes 4096
  121.1 5.6 %psum.7 = f32[64]{0:T(128)S(1)} all-reduce(f32[64]{0:T(128)S(1)} %dynamic-slice.4), channel_id=1, replica_groups=mesh['dp'=8,'seq'=4] {'seq'}, use_global_device_ids=true, to_apply=%region_9.10 | all-reduce | flops 64 | bytes 512 | tf_op jit(solution)/shard_map/psum | solution.py:206
  127.2 1.2 copy.58
  (44 shorter events, 8.3 us)
Async XLA Ops:
  0.6 31.9 %copy-start.2 = (bf16[1,128,4,128]{3,2,1,0:T(4,128)(2,1)S(1)}, bf16[1,128,4,128]{3,2,1,0:T(4,128)(2,1)}, u32[]{:S(2)}) copy-start(bf16[1,128,4,128]{3,2,1,0:T(4,128)(2,1)} %param.11) | copy-start | bytes 393220
  0.6 32.6 %copy-start.3 = (s32[1,128]{1,0:T(1,128)S(1)}, s32[1,128]{1,0:T(1,128)}, u32[]{:S(2)}) copy-start(s32[1,128]{1,0:T(1,128)} %param.13) | copy-start | bytes 1540
  2.3 8.9 %all-to-all-start = ((bf16[128,4,128]{2,0,1:T(8,128)(2,1)}), bf16[128,4,128]{2,0,1:T(8,128)(2,1)S(1)}, u32[]{:S(2)}, u32[]{:S(2)}) async-start(bf16[128,4,128]{2,0,1:T(8,128)(2,1)} %bitcast.125), calls=%async_computation | async-start | bytes 262144 | tf_op jit(solution)/shard_map/all_to_all | solution.py:54
  11.1 17.9 %all-to-all-start.1 = ((bf16[128,32,128]{2,0,1:T(8,128)(2,1)}), bf16[128,32,128]{2,0,1:T(8,128)(2,1)S(1)}, u32[]{:S(2)}, u32[]{:S(2)}) async-start(bf16[128,32,128]{2,0,1:T(8,128)(2,1)} %bitcast.123), calls=%async_computation.1 | async-start | bytes 2097152 | tf_op jit(solution)/shard_map/all_to_all | solution.py:50
  29.1 18.8 %all-to-all-start.3 = ((bf16[128,32,128]{2,0,1:T(8,128)(2,1)}), bf16[128,32,128]{2,0,1:T(8,128)(2,1)S(1)}, u32[]{:S(2)}, u32[]{:S(2)}) async-start(bf16[128,32,128]{2,0,1:T(8,128)(2,1)} %bitcast.122), calls=%async_computation.3 | async-start | bytes 2097152 | tf_op jit(solution)/shard_map/all_to_all | solution.py:51
  47.9 7.9 %all-to-all-start.2 = ((bf16[128,4,128]{2,0,1:T(8,128)(2,1)}), bf16[128,4,128]{2,0,1:T(8,128)(2,1)S(1)}, u32[]{:S(2)}, u32[]{:S(2)}) async-start(bf16[128,4,128]{2,0,1:T(8,128)(2,1)} %bitcast.124), calls=%async_computation.2 | async-start | bytes 262144 | tf_op jit(solution)/shard_map/all_to_all | solution.py:61
  64.3 31.4 %copy-start.4 = (u32[32]{0:T(128)S(1)}, u32[32]{0:T(128)}, u32[]{:S(2)}) copy-start(u32[32]{0:T(128)} %constant.142) | copy-start | bytes 388
  68.9 2.6 %copy-start = (f32[512,8,128]{2,0,1:T(8,128)S(1)}, f32[512,8,128]{2,0,1:T(8,128)}, u32[]{:S(2)}) copy-start(f32[512,8,128]{2,0,1:T(8,128)} %get-tuple-element.768) | copy-start | bytes 6291460 | tf_op jit(solution)/shard_map/while/body/eval_jaxpr/while
  73.1 1.3 %copy-start.1 = (f32[512,8,128]{2,0,1:T(8,128)}, f32[512,8,128]{2,0,1:T(8,128)S(1)}, u32[]{:S(2)}) copy-start(f32[512,8,128]{2,0,1:T(8,128)S(1)} %bitcast_add_fusion.2) | copy-start | bytes 6291460 | tf_op jit(solution)/shard_map/while/body/eval_jaxpr/while
  76.4 7.9 %all-to-all-start.5 = ((bf16[4,2,8192]{2,1,0:T(2,128)(2,1)}), bf16[4,2,8192]{2,1,0:T(2,128)(2,1)S(1)}, u32[]{:S(2)}, u32[]{:S(2)}) async-start(bf16[4,2,8192]{2,1,0:T(2,128)(2,1)} %reshape.211), calls=%async_computation.5 | async-start | bytes 262144 | tf_op jit(solution)/shard_map/all_to_all | solution.py:195
  84.3 7.9 %all-to-all-start.6 = ((bf16[4,2,8192]{2,1,0:T(2,128)(2,1)}), bf16[4,2,8192]{2,1,0:T(2,128)(2,1)S(1)}, u32[]{:S(2)}, u32[]{:S(2)}) async-start(bf16[4,2,8192]{2,1,0:T(2,128)(2,1)} %reshape.213), calls=%async_computation.6 | async-start | bytes 262144 | tf_op jit(solution)/shard_map/all_to_all | solution.py:196
  92.2 35.0 %all-to-all-start.4 = ((bf16[512,8,128]{2,1,0:T(8,128)(2,1)}), bf16[512,8,128]{2,1,0:T(8,128)(2,1)S(1)}, u32[]{:S(2)}, u32[]{:S(2)}) async-start(bf16[512,8,128]{2,1,0:T(8,128)(2,1)} %fusion.26), calls=%async_computation.4 | async-start | bytes 2097152 | tf_op jit(solution)/shard_map/all_to_all | solution.py:194
where the time goes:
time: 129 us; the launch traced here: 128 us
  blocking collectives  42.4 us (33%)
  starting transfers between devices  24.8 us (19%)
  waiting for transfers between devices  20.1 us (16%)
  local copies, waits for them, and re-layouts  16.7 us (13%)
  matrix products  13 us (10%)
  other arithmetic  8.5 us (7%)
  between operations  2.77 us (2%)
    unnamed x1, blocking collectives  22.1 us
    all_gather x1, blocking collectives, shards(): documents_per_row = lax.all_gather(doc_ids[0], 'seq', axis=0, tiled=True)  14.6 us
    all_to_all x1, waiting for transfers between devices, shards(): lax.all_to_all(query_local, 'seq', split_axis=1, concat_axis=0, tiled=True)  11.8 us
    unnamed x20, local copies, waits for them, and re-layouts  11.4 us
    psum x1, blocking collectives, shards(): total_bias = lax.psum(row_bias, 'seq')  5.63 us
    dot_general x2, matrix products, tile_terms(): jnp.einsum('qhd,kd->hqk', query_block, block_of_keys, preferred_element_t...  4.44 us
    dot_general x2, matrix products, tile_terms(): jnp.einsum('qhd,kd->hqk', grad_block, block_of_values, preferred_element_...  4.28 us
    all_to_all x1, starting transfers between devices, shards(): lax.all_to_all(jnp.repeat(key_local, head_copies, axis=1), 'seq', split_a...  4.26 us
  transfers between devices with their start and end apart: 7, of which 5 were waited for; matrix products, arithmetic and copies ran while one was open for 12% of the time, Pallas kernels for 0%

commit v1 on v0

--- a/solution.py
+++ b/solution.py
@@ -47,7 +47,12 @@
     head_copies = seq_size // kv_heads
     documents_per_row = lax.all_gather(doc_ids[0], "seq", axis=0, tiled=True)
     query_row, grad_row = (
-        lax.all_to_all(query_local, "seq", split_axis=1, concat_axis=0, tiled=True),
+        jnp.concatenate(
+            lax.all_to_all(
+                jnp.stack(jnp.split(query_local, lax.axis_size("seq"), axis=1)), "seq", 0, 0
+            ),
+            axis=0,
+        ),
         lax.all_to_all(grad_local, "seq", split_axis=1, concat_axis=0, tiled=True),
     )
     key_copies, value_copies = (

time: 129 us -> 129 us (level)
    all_to_all x1, waiting for transfers between devices: 0.01 us -> 12 us  [shards(): lax.all_to_all(grad_local, 'seq', split_axis=1, concat_axis=0, tiled=True)]
    all_to_all x1, waiting for transfers between devices: 11.8 us -> 0.01 us  [shards(): lax.all_to_all(jnp.stack(jnp.split(query_local, lax.axis_size('seq'), axi...]
    unnamed x20 -> x19, local copies, waits for them, and re-layouts: 11.4 us -> 8.75 us
    another operation x6 -> x7, local copies, waits for them, and re-layouts: 1.56 us -> 2.84 us
where the time goes in v1:
time: 129 us; the launch traced here: 128 us
  blocking collectives  42.4 us (33%)
  starting transfers between devices  24.8 us (19%)
  waiting for transfers between devices  20.2 us (16%)
  local copies, waits for them, and re-layouts  15.5 us (12%)
  matrix products  13 us (10%)
  other arithmetic  9.6 us (7%)
  between operations  2.78 us (2%)
    unnamed x1, blocking collectives  22.1 us
    all_gather x1, blocking collectives, shards(): documents_per_row = lax.all_gather(doc_ids[0], 'seq', axis=0, tiled=True)  14.6 us
    all_to_all x1, waiting for transfers between devices, shards(): lax.all_to_all(grad_local, 'seq', split_axis=1, concat_axis=0, tiled=True)  12 us
    unnamed x19, local copies, waits for them, and re-layouts  8.75 us
    psum x1, blocking collectives, shards(): total_bias = lax.psum(row_bias, 'seq')  5.63 us
    dot_general x2, matrix products, tile_terms(): jnp.einsum('qhd,kd->hqk', query_block, block_of_keys, preferred_element_t...  4.44 us
    dot_general x2, matrix products, tile_terms(): jnp.einsum('qhd,kd->hqk', grad_block, block_of_values, preferred_element_...  4.28 us
    all_to_all x1, starting transfers between devices, shards(): lax.all_to_all(jnp.repeat(key_local, head_copies, axis=1), 'seq', split_a...  4.26 us
  transfers between devices with their start and end apart: 7, of which 5 were waited for; matrix products, arithmetic and copies ran while one was open for 12% of the time, Pallas kernels for 0%

profile of v1, /device:TPU:0, one launch (start us, length us, event | category | flops | bytes accessed | tf_op | source)
XLA Modules:
  0.0 128.4 jit_solution(1781094178856411546)
XLA Ops:
  0.7 1.6 %copy.58 = bf16[1,128,4,128]{3,1,2,0:T(8,128)(2,1)} copy(bf16[1,128,4,128]{3,2,1,0:T(4,128)(2,1)} %param.10) | data formatting | bytes 262144 | tf_op args[1]
  2.3 4.3 %all-to-all-start = ((bf16[128,4,128]{2,0,1:T(8,128)(2,1)}), bf16[128,4,128]{2,0,1:T(8,128)(2,1)S(1)}, u32[]{:S(2)}, u32[]{:S(2)}) async-start(bf16[128,4,128]{2,0,1:T(8,128)(2,1)} %bitcast.128), calls=%async_computation | async-start | bytes 262144 | tf_op jit(solution)/shard_map/all_to_all | solution.py:59
  6.5 2.6 %copy.56 = bf16[1,128,32,128]{3,1,2,0:T(8,128)(2,1)} copy(bf16[1,128,32,128]{3,2,1,0:T(8,128)(2,1)} %param.12) | data formatting | bytes 2097152 | tf_op args[3]
  9.1 2.0 %all-to-all-done = bf16[128,4,128]{2,0,1:T(8,128)(2,1)S(1)} async-done(((bf16[128,4,128]{2,0,1:T(8,128)(2,1)}), bf16[128,4,128]{2,0,1:T(8,128)(2,1)S(1)}, u32[]{:S(2)}, u32[]{:S(2)}) %all-to-all-start) | async-done | bytes 131104 | tf_op jit(solution)/shard_map/all_to_all | solution.py:59
  11.1 3.5 %all-to-all-start.3 = ((bf16[128,32,128]{2,0,1:T(8,128)(2,1)}), bf16[128,32,128]{2,0,1:T(8,128)(2,1)S(1)}, u32[]{:S(2)}, u32[]{:S(2)}) async-start(bf16[128,32,128]{2,0,1:T(8,128)(2,1)} %bitcast.126), calls=%async_computation.3 | async-start | bytes 2097152 | tf_op jit(solution)/shard_map/all_to_all | solution.py:56
  14.7 1.3 %slice_bitcast_fusion.3 = (bf16[1,128,8,128]{3,2,1,0:T(8,128)(2,1)S(1)}, bf16[1,128,8,128]{3,2,1,0:T(8,128)(2,1)S(1)}, bf16[1,128,8,128]{3,2,1,0:T(8,128)(2,1)S(1)}, bf16[1,128,8,128]{3,2,1,0:T(8,128)(2,1)S(1)}) fusion(bf16[128,32,128]{2,1,0:T(8,128)(2,1)} %bitcast.189), kind=kLoop, calls=%fused_computation.44 | loop fusion | bytes 2097152 | tf_op jit(solution)/shard_map/stack | solution.py:52
  16.0 1.1 pad_maximum_fusion
  17.1 12.0 %all-to-all-done.3 = bf16[128,32,128]{2,0,1:T(8,128)(2,1)S(1)} async-done(((bf16[128,32,128]{2,0,1:T(8,128)(2,1)}), bf16[128,32,128]{2,0,1:T(8,128)(2,1)S(1)}, u32[]{:S(2)}, u32[]{:S(2)}) %all-to-all-start.3) | async-done | bytes 1048608 | tf_op jit(solution)/shard_map/all_to_all | solution.py:56
  29.1 3.5 %all-to-all-start.1 = ((bf16[4,128,8,128]{3,2,1,0:T(8,128)(2,1)}), bf16[4,128,8,128]{3,2,1,0:T(8,128)(2,1)S(1)}, u32[]{:S(2)}, u32[]{:S(2)}) async-start(bf16[4,128,8,128]{3,2,1,0:T(8,128)(2,1)} %pad_maximum_fusion), calls=%async_computation.1 | async-start | bytes 2097152 | tf_op jit(solution)/shard_map/all_to_all | solution.py:51
  33.3 14.6 %all-gather = s32[1,512]{1,0:T(1,128)S(1)} all-gather(s32[1,128]{1,0:T(1,128)S(1)} %copy-done.3), channel_id=2, replica_groups=mesh['dp'=8,'seq'=4] {'seq'}, dimensions={1}, use_global_device_ids=true | all-gather | bytes 2560 | tf_op jit(solution)/shard_map/all_gather | solution.py:48
  47.9 3.3 %all-to-all-start.2 = ((bf16[128,4,128]{2,0,1:T(8,128)(2,1)}), bf16[128,4,128]{2,0,1:T(8,128)(2,1)S(1)}, u32[]{:S(2)}, u32[]{:S(2)}) async-start(bf16[128,4,128]{2,0,1:T(8,128)(2,1)} %bitcast.127), calls=%async_computation.2 | async-start | bytes 262144 | tf_op jit(solution)/shard_map/all_to_all | solution.py:66
  53.5 2.3 %all-to-all-done.2 = bf16[128,4,128]{2,0,1:T(8,128)(2,1)S(1)} async-done(((bf16[128,4,128]{2,0,1:T(8,128)(2,1)}), bf16[128,4,128]{2,0,1:T(8,128)(2,1)S(1)}, u32[]{:S(2)}, u32[]{:S(2)}) %all-to-all-start.2) | async-done | bytes 131104 | tf_op jit(solution)/shard_map/all_to_all | solution.py:66
  55.8 6.9 %while.59 = (s32[]{:T(128)}, f32[8,512]{1,0:T(8,128)S(1)}, f32[8,512]{1,0:T(8,128)S(1)}, f32[8,512]{1,0:T(8,128)S(1)}, s32[512]{0:T(512)S(1)}, /*index=5*/bf16[5...) while((s32[]{:T(128)}, f32[8,512]{1,0:T(8,128)S(1)}, ...), condition=%wide.region_4.0_spmd, body=%wide.region_0.4_spmd.sunk | while | flops 1103901184 | bytes 28874876 | solution.py:120
  56.1 1.5 %fusion.63 = (f32[8,512]{1,0:T(8,128)S(1)}, f32[512,512,8]{1,0,2:T(8,128)S(1)}) fusion(pred[512,512]{0,1:T(8,128)(4,1)S(1)} %fusion.62, bf16[512,8,128]{2,0,1:T(8,128)(2,1)S(1)} %get-tuple-element.752, bf16[512,128]{1,0:T(8,128)(2,1)S(1)} %get-tuple-element.751), kind=kOutput, calls=%fused_computation.4.clone.1 | convolution fusion | flops 543158272 | bytes 9846784 | tf_op jit(solution)/shard_map/while/body/eval_jaxpr/while/body/qhd,kd->hqk/dot_general | solution.py:22
  57.7 2.0 %fusion.65 = f32[8,512]{1,0:T(8,128)S(1)} fusion(f32[512,512,8]{1,0,2:T(8,128)S(1)} %get-tuple-element.709, f32[8,512]{1,0:T(8,128)S(1)} %max.9, pred[512,512]{0,1:T(8,128)(4,1)S(1)} %fusion.62), kind=kLoop, calls=%fused_computation.5.clone.1 | loop fusion | flops 10481664 | bytes 8683520 | tf_op jit(solution)/shard_map/while/body/eval_jaxpr/while/body/reduce_sum | solution.py:110
  59.7 3.0 %fusion.64 = f32[8,512]{1,0:T(8,128)S(1)} fusion(f32[512,512,8]{1,0,2:T(8,128)S(1)} %get-tuple-element.709, f32[8,512]{1,0:T(8,128)S(1)} %max.9, pred[512,512]{0,1:T(8,128)(4,1)S(1)} %fusion.62, bf16[512,8,128]{2,0,1:T(8,128)(2,1)S(1)} %get-tuple-element.754, bf16[512,128]{1,0:T(8,128)(2,1)S(1)} %get-tuple-element.753), kind=kOutput, calls=%fused_computation.1.clone.1 | convolution fusion | flops 549449728 | bytes 9863168 | tf_op jit(solution)/shard_map/while/body/eval_jaxpr/while/body/qhd,kd->hqk/dot_general | solution.py:25
  62.8 1.5 %broadcast.192 = f32[512,8,128]{2,0,1:T(8,128)} broadcast(f32[]{:T(128)} %constant.131.clone.1), dimensions={} | broadcast | bytes 2097156 | tf_op jit(solution)/shard_map/broadcast.14
  64.3 10.2 %while.60 = (s32[]{:T(128)}, f32[512,8,128]{2,0,1:T(8,128)}, f32[512,128]{1,0:T(8,128)S(1)}, f32[512,128]{1,0:T(8,128)S(1)}, s32[512]{0:T(512)S(1)}, /*index=5*/...) while((s32[]{:T(128)}, f32[512,8,128]{2,0,1:T(8,128)}, ...), condition=%wide.region_6.7_spmd, body=%wide.region_5.0_spmd.sunk | while | flops 2704671232 | bytes 64936140 | solution.py:181
  64.6 2.9 %fusion.77 = f32[8,512,512]{1,2,0:T(8,128)S(1)} fusion(f32[8,512]{1,0:T(8,128)S(1)} %bitcast.193, f32[8,512]{1,0:T(8,128)S(1)} %bitcast.186, pred[512,512]{0,1:T(8,128)(4,1)S(1)} %fusion.76, bf16[512,8,128]{2,0,1:T(8,128)(2,1)S(1)} %get-tuple-element.791, bf16[512,128]{1,0:T(8,128)(2,1)S(1)} %get-tuple-element.790), kind=kOutput, calls=%fused_computation.22.clone.1 | convolution fusion | flops 547356672 | bytes 9863168 | tf_op jit(solution)/shard_map/while/body/eval_jaxpr/while/body/qhd,kd->hqk/dot_general | solution.py:22
  67.5 1.3 %fusion.80 = f32[512,128]{1,0:T(8,128)S(1)} fusion(f32[512,128]{1,0:T(8,128)S(1)} %get-tuple-element.774, bf16[512,8,128]{2,0,1:T(8,128)(2,1)S(1)} %get-tuple-element.795, f32[8,512,512]{1,2,0:T(8,128)S(1)} %fusion.77), kind=kOutput, calls=%fused_computation.28.clone.1 | convolution fusion | flops 539033600 | bytes 9961472 | tf_op jit(solution)/shard_map/while/body/eval_jaxpr/while/body/hqk,qhd->kd/dot_general | solution.py:163
  68.9 1.3 %fusion.78 = bf16[8,512,512]{1,2,0:T(8,128)(2,1)S(1)} fusion(f32[8,512,512]{1,2,0:T(8,128)S(1)} %fusion.77, f32[8,512]{1,0:T(8,128)S(1)} %bitcast.194, bf16[512,8,128]{2,0,1:T(8,128)(2,1)S(1)} %get-tuple-element.795, bf16[512,128]{1,0:T(8,128)(2,1)S(1)} %get-tuple-element.794), kind=kOutput, calls=%fused_computation.17.clone.1 | convolution fusion | flops 543162368 | bytes 13778944 | tf_op jit(solution)/shard_map/while/body/eval_jaxpr/while/body/qhd,kd->hqk/dot_general | solution.py:25
  70.2 1.3 fusion.79
  71.5 1.7 %bitcast_add_fusion.2 = f32[512,8,128]{2,0,1:T(8,128)S(1)} fusion(f32[512,8,128]{2,0,1:T(8,128)S(1)} %copy-done, bf16[8,512,512]{1,2,0:T(8,128)(2,1)S(1)} %fusion.78, bf16[512,128]{1,0:T(8,128)(2,1)S(1)} %get-tuple-element.790), kind=kOutput, calls=%fused_computation.25.clone.1 | convolution fusion | flops 537395200 | bytes 8519680 | tf_op jit(solution)/shard_map/while/body/eval_jaxpr/while/body/hqk,kd->qhd/dot_general | solution.py:157
  73.1 1.3 %copy-done.1 = f32[512,8,128]{2,0,1:T(8,128)} copy-done((f32[512,8,128]{2,0,1:T(8,128)}, f32[512,8,128]{2,0,1:T(8,128)S(1)}, u32[]{:S(2)}) %copy-start.1) | copy-done | bytes 2097176 | tf_op jit(solution)/shard_map/while/body/eval_jaxpr/while
  76.4 3.3 %all-to-all-start.5 = ((bf16[4,2,8192]{2,1,0:T(2,128)(2,1)}), bf16[4,2,8192]{2,1,0:T(2,128)(2,1)S(1)}, u32[]{:S(2)}, u32[]{:S(2)}) async-start(bf16[4,2,8192]{2,1,0:T(2,128)(2,1)} %reshape.215), calls=%async_computation.5 | async-start | bytes 262144 | tf_op jit(solution)/shard_map/all_to_all | solution.py:200
  81.1 3.2 %all-to-all-done.5 = bf16[4,2,8192]{2,1,0:T(2,128)(2,1)S(1)} async-done(((bf16[4,2,8192]{2,1,0:T(2,128)(2,1)}), bf16[4,2,8192]{2,1,0:T(2,128)(2,1)S(1)}, u32[]{:S(2)}, u32[]{:S(2)}) %all-to-all-start.5) | async-done | bytes 131104 | tf_op jit(solution)/shard_map/all_to_all | solution.py:200
  84.3 3.3 %all-to-all-start.6 = ((bf16[4,2,8192]{2,1,0:T(2,128)(2,1)}), bf16[4,2,8192]{2,1,0:T(2,128)(2,1)S(1)}, u32[]{:S(2)}, u32[]{:S(2)}) async-start(bf16[4,2,8192]{2,1,0:T(2,128)(2,1)} %reshape.217), calls=%async_computation.6 | async-start | bytes 262144 | tf_op jit(solution)/shard_map/all_to_all | solution.py:201
  87.6 3.9 %fusion.26 = bf16[512,8,128]{2,1,0:T(8,128)(2,1)} fusion(f32[512,8,128]{2,0,1:T(8,128)} %get-tuple-element.519), kind=kLoop, calls=%fused_computation.37 | loop fusion | flops 1048576 | bytes 3145728 | tf_op jit(solution)/shard_map/convert_element_type | solution.py:195
  92.2 3.5 %all-to-all-start.4 = ((bf16[512,8,128]{2,1,0:T(8,128)(2,1)}), bf16[512,8,128]{2,1,0:T(8,128)(2,1)S(1)}, u32[]{:S(2)}, u32[]{:S(2)}) async-start(bf16[512,8,128]{2,1,0:T(8,128)(2,1)} %fusion.26), calls=%async_computation.4 | async-start | bytes 2097152 | tf_op jit(solution)/shard_map/all_to_all | solution.py:199
  98.9 22.1 %all-reduce = f32[512]{0:T(512)S(1)} all-reduce(f32[512]{0:T(512)S(1)} %bitcast.196), channel_id=3, replica_groups=mesh['dp'=8,'seq'=4] {'dp'}, use_global_device_ids=true, to_apply=%region_8.9.clone | all-reduce | flops 512 | bytes 4096
  121.1 5.6 %psum.7 = f32[64]{0:T(128)S(1)} all-reduce(f32[64]{0:T(128)S(1)} %dynamic-slice.4), channel_id=1, replica_groups=mesh['dp'=8,'seq'=4] {'seq'}, use_global_device_ids=true, to_apply=%region_9.10 | all-reduce | flops 64 | bytes 512 | tf_op jit(solution)/shard_map/psum | solution.py:211
  127.2 1.2 copy.55
  (45 shorter events, 9.2 us)
Async XLA Ops:
  0.6 31.9 %copy-start.2 = (bf16[1,128,4,128]{3,2,1,0:T(4,128)(2,1)S(1)}, bf16[1,128,4,128]{3,2,1,0:T(4,128)(2,1)}, u32[]{:S(2)}) copy-start(bf16[1,128,4,128]{3,2,1,0:T(4,128)(2,1)} %param.11) | copy-start | bytes 393220
  0.6 32.6 %copy-start.3 = (s32[1,128]{1,0:T(1,128)S(1)}, s32[1,128]{1,0:T(1,128)}, u32[]{:S(2)}) copy-start(s32[1,128]{1,0:T(1,128)} %param.13) | copy-start | bytes 1540
  2.3 8.9 %all-to-all-start = ((bf16[128,4,128]{2,0,1:T(8,128)(2,1)}), bf16[128,4,128]{2,0,1:T(8,128)(2,1)S(1)}, u32[]{:S(2)}, u32[]{:S(2)}) async-start(bf16[128,4,128]{2,0,1:T(8,128)(2,1)} %bitcast.128), calls=%async_computation | async-start | bytes 262144 | tf_op jit(solution)/shard_map/all_to_all | solution.py:59
  11.1 17.9 %all-to-all-start.3 = ((bf16[128,32,128]{2,0,1:T(8,128)(2,1)}), bf16[128,32,128]{2,0,1:T(8,128)(2,1)S(1)}, u32[]{:S(2)}, u32[]{:S(2)}) async-start(bf16[128,32,128]{2,0,1:T(8,128)(2,1)} %bitcast.126), calls=%async_computation.3 | async-start | bytes 2097152 | tf_op jit(solution)/shard_map/all_to_all | solution.py:56
  29.1 18.8 %all-to-all-start.1 = ((bf16[4,128,8,128]{3,2,1,0:T(8,128)(2,1)}), bf16[4,128,8,128]{3,2,1,0:T(8,128)(2,1)S(1)}, u32[]{:S(2)}, u32[]{:S(2)}) async-start(bf16[4,128,8,128]{3,2,1,0:T(8,128)(2,1)} %pad_maximum_fusion), calls=%async_computation.1 | async-start | bytes 2097152 | tf_op jit(solution)/shard_map/all_to_all | solution.py:51
  47.9 7.9 %all-to-all-start.2 = ((bf16[128,4,128]{2,0,1:T(8,128)(2,1)}), bf16[128,4,128]{2,0,1:T(8,128)(2,1)S(1)}, u32[]{:S(2)}, u32[]{:S(2)}) async-start(bf16[128,4,128]{2,0,1:T(8,128)(2,1)} %bitcast.127), calls=%async_computation.2 | async-start | bytes 262144 | tf_op jit(solution)/shard_map/all_to_all | solution.py:66
  64.3 31.4 %copy-start.4 = (u32[32]{0:T(128)S(1)}, u32[32]{0:T(128)}, u32[]{:S(2)}) copy-start(u32[32]{0:T(128)} %constant.142) | copy-start | bytes 388
  68.8 2.6 %copy-start = (f32[512,8,128]{2,0,1:T(8,128)S(1)}, f32[512,8,128]{2,0,1:T(8,128)}, u32[]{:S(2)}) copy-start(f32[512,8,128]{2,0,1:T(8,128)} %get-tuple-element.772) | copy-start | bytes 6291460 | tf_op jit(solution)/shard_map/while/body/eval_jaxpr/while
  73.1 1.3 %copy-start.1 = (f32[512,8,128]{2,0,1:T(8,128)}, f32[512,8,128]{2,0,1:T(8,128)S(1)}, u32[]{:S(2)}) copy-start(f32[512,8,128]{2,0,1:T(8,128)S(1)} %bitcast_add_fusion.2) | copy-start | bytes 6291460 | tf_op jit(solution)/shard_map/while/body/eval_jaxpr/while
  76.4 7.9 %all-to-all-start.5 = ((bf16[4,2,8192]{2,1,0:T(2,128)(2,1)}), bf16[4,2,8192]{2,1,0:T(2,128)(2,1)S(1)}, u32[]{:S(2)}, u32[]{:S(2)}) async-start(bf16[4,2,8192]{2,1,0:T(2,128)(2,1)} %reshape.215), calls=%async_computation.5 | async-start | bytes 262144 | tf_op jit(solution)/shard_map/all_to_all | solution.py:200
  84.3 7.9 %all-to-all-start.6 = ((bf16[4,2,8192]{2,1,0:T(2,128)(2,1)}), bf16[4,2,8192]{2,1,0:T(2,128)(2,1)S(1)}, u32[]{:S(2)}, u32[]{:S(2)}) async-start(bf16[4,2,8192]{2,1,0:T(2,128)(2,1)} %reshape.217), calls=%async_computation.6 | async-start | bytes 262144 | tf_op jit(solution)/shard_map/all_to_all | solution.py:201
  92.2 35.0 %all-to-all-start.4 = ((bf16[512,8,128]{2,1,0:T(8,128)(2,1)}), bf16[512,8,128]{2,1,0:T(8,128)(2,1)S(1)}, u32[]{:S(2)}, u32[]{:S(2)}) async-start(bf16[512,8,128]{2,1,0:T(8,128)(2,1)} %fusion.26), calls=%async_computation.4 | async-start | bytes 2097152 | tf_op jit(solution)/shard_map/all_to_all | solution.py:199
